TPU v7x, 256 devices: a whole 4x4x8 slice. The times are simulated.
256 devices in a mesh: pts: 128 (over y, x, z_lo, core), grp: 2 (over z_hi).
Axes of the slice: x: 4, y: 4, z: 8 (z_hi: 2, z_lo: 4; z = z_hi * 4 + z_lo), core: 2. Of those that a mesh axis runs over, the one named last changes fastest.
Arguments:
- grid_states: float32 [59, 2097152], P(None, ('pts', 'grp')), may hold values from 0 to 1
- coarse_active: int32 [16384, 8], P(('pts', 'grp')), may hold values from 0 to 127, all different within a row
- fine_active: int32 [16384, 8], P(('pts', 'grp')), may hold values from 0 to 31, all different within a row
- shock: int32 [2097152], P(('pts', 'grp')), may hold values from 0 to 3
- coarse_surplus: bfloat16 [4, 60, 16384], P(None, 'grp', 'pts'), may hold values from -0.796875 to 0.796875
- fine_surplus: bfloat16 [4, 60, 524288], P(None, 'grp', 'pts'), may hold values from -0.796875 to 0.796875
- coarse_dim: int32 [128], P('pts'), may hold values from 0 to 58
- coarse_level: int32 [128], P('pts'), may hold values from 0 to 2
- fine_dim: int32 [4096], P('pts'), may hold values from 0 to 58
- fine_level: int32 [4096], P('pts'), may hold values from 0 to 2
- tfp: float32 [4], replicated, may hold values from 0.5 to 2
- trans_weight: float32 [4, 4], replicated, may hold values from 0.2 to 5
Outputs:
- savings: bfloat16 [4, 60, 2097152], P(None, None, ('pts', 'grp'))
- prices: float32 [2, 2097152], P(None, ('pts', 'grp'))
Inputs may be any that keep to these rules, and one draw needn't show every extreme that they name: `coarse_active`: each row names 8 different coarse blocks, and every coarse block is named by some row. `fine_active`: each row names 8 different fine blocks of its region.
All inputs are finite; a program needn't handle non-finite values.
Results may differ from a plain program's by a relative error of at most 0.0034.
Values may be sent and summed in bfloat16 or wider, within the bound.
A program may use at most 128 MiB of HBM per device.

v0:
```python
import math
import jax
import jax.numpy as jnp
from jax import lax
from jax.sharding import PartitionSpec as P

S = 4
GEN = 60
BS = 128


def evaluate(states, active, table, dims_all, levels_all):
    nstate, npoints = states.shape
    tiles, nactive = active.shape
    tile = npoints // tiles
    block_size = table.shape[2]
    turns = math.gcd(tiles, 8)
    group = tiles // turns
    grouped = states.reshape(nstate, turns, group, tile).transpose(1, 2, 0, 3)
    active_grouped = active.reshape(turns, group, nactive)
    offsets = jnp.arange(block_size, dtype=jnp.float32)

    def one_tile(states_tile, block_ids):
        scales = (block_size - 1) * jnp.exp2(-levels_all[block_ids].astype(jnp.float32))
        scaled = scales[:, None] * states_tile[dims_all[block_ids]]
        phi = jnp.maximum(0.0, 1.0 - jnp.abs(scaled[:, None, :] - offsets[None, :, None])).astype(
            jnp.bfloat16
        )
        coef = table[block_ids]
        return jnp.einsum("kgj,kjt->gt", coef, phi, preferred_element_type=jnp.float32)

    def one_turn(pair):
        return jax.vmap(one_tile)(pair[0], pair[1])

    values = lax.map(one_turn, (grouped, active_grouped))
    return values.transpose(2, 0, 1, 3).reshape(table.shape[1], npoints)


def to_table(gathered):
    shocks, gens, basis = gathered.shape
    nblocks = basis // BS
    return gathered.reshape(shocks * gens, nblocks, BS).transpose(1, 0, 2)


def joined(coarse_all, fine_local, coarse_ids, fine_ids):
    table = jnp.concatenate([to_table(coarse_all), to_table(fine_local)], axis=0)
    ncoarse = coarse_all.shape[2] // BS
    ids = jnp.concatenate([coarse_ids, fine_ids + ncoarse], axis=1)
    return (table, ids)


def expected_prices(savings, shock, tfp, trans_weight):
    capital = jnp.mean(savings.astype(jnp.float32), axis=1)
    interest = 0.33 * tfp[:, None] * capital ** (0.33 - 1.0) + 1.0 - 0.1
    earnings = (1.0 - 0.33) * tfp[:, None] * capital**0.33
    transition = trans_weight / jnp.sum(trans_weight, axis=1, keepdims=True)
    onehot = (shock[None, :] == jnp.arange(S, dtype=jnp.int32)[:, None]).astype(jnp.float32)
    weights = jnp.dot(transition.T, onehot, precision=lax.Precision.HIGHEST)
    return jnp.stack([jnp.sum(weights * interest, axis=0), jnp.sum(weights * earnings, axis=0)])


def body(
    grid_states,
    coarse_active,
    fine_active,
    shock,
    coarse_surplus,
    fine_surplus,
    coarse_dim,
    coarse_level,
    fine_dim,
    fine_level,
    tfp,
    trans_weight,
):
    npoints = grid_states.shape[1]
    coarse_gens, fine_gens = (
        lax.all_gather(coarse_surplus, "grp", axis=1, tiled=True),
        lax.all_gather(fine_surplus, "grp", axis=1, tiled=True),
    )
    coarse_all, dims_coarse, levels_coarse = (
        lax.all_gather(coarse_gens, "pts", axis=2, tiled=True),
        lax.all_gather(coarse_dim, "pts", axis=0, tiled=True),
        lax.all_gather(coarse_level, "pts", axis=0, tiled=True),
    )
    table, block_ids = joined(coarse_all, fine_gens, coarse_active, fine_active)
    dims_all = jnp.concatenate([dims_coarse, fine_dim])
    levels_all = jnp.concatenate([levels_coarse, fine_level])
    log_savings = evaluate(grid_states, block_ids, table, dims_all, levels_all)
    savings = jnp.exp(log_savings).astype(jnp.bfloat16).reshape(S, GEN, npoints)
    prices = expected_prices(savings, shock, tfp, trans_weight)
    return (savings, prices)


def solution(mesh):
    in_specs = (
        P(None, ("pts", "grp")),
        P(("pts", "grp"), None),
        P(("pts", "grp"), None),
        P(("pts", "grp")),
        P(None, "grp", "pts"),
        P(None, "grp", "pts"),
        P("pts"),
        P("pts"),
        P("pts"),
        P("pts"),
        P(),
        P(),
    )
    out_specs = (P(None, None, ("pts", "grp")), P(None, ("pts", "grp")))
    return jax.shard_map(body, mesh=mesh, in_specs=in_specs, out_specs=out_specs, check_vma=False)
```

profile of v0, /device:TPU:1, one launch (start us, length us, event | category | flops | bytes accessed | tf_op | source)
XLA Modules:
  0.0 540.3 jit_solution(2822092789721412001)
XLA Ops:
  7.9 11.4 %all_gather.15 = bf16[4,60,128]{2,0,1:T(4,128)(2,1)} all-gather(bf16[4,30,128]{2,0,1:T(4,128)(2,1)} %param.18), channel_id=1, replica_groups=mesh['pts'=128,'grp'=2] {'grp'}, dimensions={1}, use_global_device_ids=true | all-gather | bytes 92160 | tf_op jit(solution)/shard_map/all_gather | solution.py:78
  20.7 2.0 copy.31
  24.2 1.3 dynamic-slice
  27.8 21.5 %all-reduce.2 = (s32[128]{0:T(128)S(1)}, s32[128]{0:T(128)S(1)}) all-reduce(s32[128]{0:T(128)S(1)} %dynamic-update-slice, s32[128]{0:T(128)S(1)} %dynamic-update-slice.1), channel_id=1, replica_groups=mesh['pts'=128,'grp'=2] {'pts'}, use_global_device_ids=true, to_apply=%add | all-reduce | flops 256 | bytes 2048
  50.6 1.5 bitcast_bitcast_fusion
  52.1 23.6 %all-gather.5.cloned.1.call-done = bf16[4,60,4096]{2,0,1:T(4,128)(2,1)} async-done(((bf16[4,30,4096]{2,0,1:T(4,128)(2,1)}), bf16[4,60,4096]{2,0,1:T(4,128)(2,1)}) %all-gather.5.cloned.1.call-update) | async-done | bytes 1966096 | tf_op jit(solution)/shard_map/all_gather | solution.py:79
  75.7 2.6 copy.24
  78.4 2.0 reshape.81
  80.4 214.3 %all-gather.3.cloned.1.call-done = bf16[4,60,16384]{2,0,1:T(4,128)(2,1)} async-done(((bf16[4,60,128]{2,0,1:T(4,128)(2,1)}), bf16[4,60,16384]{2,0,1:T(4,128)(2,1)}) %all-gather.3.cloned.1.call-update) | async-done | bytes 7864336 | tf_op jit(solution)/shard_map/all_gather | solution.py:82
  294.6 10.9 %copy.23 = bf16[4,60,16384]{2,1,0:T(8,128)(2,1)} copy(bf16[4,60,16384]{2,0,1:T(4,128)(2,1)} %all-gather.3.cloned.1.call-done) | data formatting | bytes 15728640 | tf_op jit(solution)/shard_map/all_gather | solution.py:82
  305.5 9.1 %reshape.80 = bf16[240,128,128]{2,1,0:T(8,128)(2,1)} reshape(bf16[4,60,16384]{2,1,0:T(8,128)(2,1)} %copy.23) | data formatting | bytes 15728640 | tf_op jit(solution)/shard_map/reshape | solution.py:42
  314.6 8.5 %pad_maximum_fusion = bf16[160,240,128]{2,0,1:T(8,128)(2,1)} fusion(bf16[32,240,128]{2,0,1:T(8,128)(2,1)S(1)} %bitcast.50, bf16[128,240,128]{2,0,1:T(8,128)(2,1)} %bitcast.49), kind=kLoop, calls=%fused_computation.27 | loop fusion | flops 19660800 | bytes 19660800 | tf_op jit(solution)/shard_map/concatenate | solution.py:46
  323.1 11.3 %copy.25 = bf16[160,240,128]{2,1,0:T(8,128)(2,1)} copy(bf16[160,240,128]{2,0,1:T(8,128)(2,1)} %pad_maximum_fusion) | data formatting | bytes 19660800
  334.5 174.7 %while.11 = (s32[]{:T(128)}, f32[8,8,240,128]{3,2,1,0:T(8,128)}, s32[8,8,16]{2,1,0:T(8,128)S(1)}, bf16[160,240,128]{2,1,0:T(8,128)(2,1)}, s32[160]{0:T(256)S(1)}...) while((s32[]{:T(128)}, f32[8,8,240,128]{3,2,1,0:T(8,128)}, ...), condition=%wide.region_1.2_spmd.clone, body=%wide.region_0.1_spmd.clone.sunk | while | flops 1017138048 | bytes 25404508 | solution.py:35
  334.6 1.3 gather_fusion.1
  336.0 1.0 dynamic-slice_bitcast_fusion.2
  337.0 1.0 gather_fusion.2
  337.9 1.3 gather_fusion.3
  339.4 10.4 %gather_fusion = bf16[128,240,128]{2,1,0:T(8,128)(2,1)} fusion(bf16[160,240,128]{2,1,0:T(8,128)(2,1)} %get-tuple-element.163, s32[1024]{0:T(1024)S(1)} %pad_clamp_fusion.2), kind=kCustom, calls=%fused_computation.clone.clone.1 | custom fusion | bytes 15729152 | tf_op jit(solution)/shard_map/while/body/eval_jaxpr/vmap()/gather | solution.py:29
  349.8 6.4 %fusion.35 = f32[8,8,240,128]{3,2,1,0:T(8,128)} fusion(f32[8,8,240,128]{3,2,1,0:T(8,128)} %get-tuple-element.153, s32[]{:T(128)} %get-tuple-element.152, bf16[8,16,240,128]{3,2,1,0:T(8,128)(2,1)} %bitcast.48, f32[8,16,128]{2,1,0:T(8,128)S(1)} %broadcast_multiply_fusion.4), kind=kOutput, calls=%fused_computation.15.clone.1 | convolution fusion | flops 1017118720 | bytes 8913408 | tf_op jit(solution)/shard_map/while/body/eval_jaxpr/vmap(kgj,kjt->gt)/dot_general | solution.py:30
  356.4 1.3 gather_fusion.1
  357.8 1.0 dynamic-slice_bitcast_fusion.2
  358.8 1.0 gather_fusion.2
  359.8 1.3 gather_fusion.3
  361.2 10.4 %gather_fusion = bf16[128,240,128]{2,1,0:T(8,128)(2,1)} fusion(bf16[160,240,128]{2,1,0:T(8,128)(2,1)} %get-tuple-element.163, s32[1024]{0:T(1024)S(1)} %pad_clamp_fusion.2), kind=kCustom, calls=%fused_computation.clone.clone.1 | custom fusion | bytes 15729152 | tf_op jit(solution)/shard_map/while/body/eval_jaxpr/vmap()/gather | solution.py:29
  371.6 6.5 %fusion.35 = f32[8,8,240,128]{3,2,1,0:T(8,128)} fusion(f32[8,8,240,128]{3,2,1,0:T(8,128)} %get-tuple-element.153, s32[]{:T(128)} %get-tuple-element.152, bf16[8,16,240,128]{3,2,1,0:T(8,128)(2,1)} %bitcast.48, f32[8,16,128]{2,1,0:T(8,128)S(1)} %broadcast_multiply_fusion.4), kind=kOutput, calls=%fused_computation.15.clone.1 | convolution fusion | flops 1017118720 | bytes 8913408 | tf_op jit(solution)/shard_map/while/body/eval_jaxpr/vmap(kgj,kjt->gt)/dot_general | solution.py:30
  378.2 1.3 gather_fusion.1
  379.7 1.0 dynamic-slice_bitcast_fusion.2
  380.6 1.0 gather_fusion.2
  381.6 1.3 gather_fusion.3
  383.1 10.4 %gather_fusion = bf16[128,240,128]{2,1,0:T(8,128)(2,1)} fusion(bf16[160,240,128]{2,1,0:T(8,128)(2,1)} %get-tuple-element.163, s32[1024]{0:T(1024)S(1)} %pad_clamp_fusion.2), kind=kCustom, calls=%fused_computation.clone.clone.1 | custom fusion | bytes 15729152 | tf_op jit(solution)/shard_map/while/body/eval_jaxpr/vmap()/gather | solution.py:29
  393.5 6.5 %fusion.35 = f32[8,8,240,128]{3,2,1,0:T(8,128)} fusion(f32[8,8,240,128]{3,2,1,0:T(8,128)} %get-tuple-element.153, s32[]{:T(128)} %get-tuple-element.152, bf16[8,16,240,128]{3,2,1,0:T(8,128)(2,1)} %bitcast.48, f32[8,16,128]{2,1,0:T(8,128)S(1)} %broadcast_multiply_fusion.4), kind=kOutput, calls=%fused_computation.15.clone.1 | convolution fusion | flops 1017118720 | bytes 8913408 | tf_op jit(solution)/shard_map/while/body/eval_jaxpr/vmap(kgj,kjt->gt)/dot_general | solution.py:30
  400.1 1.3 gather_fusion.1
  401.5 1.0 dynamic-slice_bitcast_fusion.2
  402.5 1.0 gather_fusion.2
  403.4 1.3 gather_fusion.3
  404.9 10.4 %gather_fusion = bf16[128,240,128]{2,1,0:T(8,128)(2,1)} fusion(bf16[160,240,128]{2,1,0:T(8,128)(2,1)} %get-tuple-element.163, s32[1024]{0:T(1024)S(1)} %pad_clamp_fusion.2), kind=kCustom, calls=%fused_computation.clone.clone.1 | custom fusion | bytes 15729152 | tf_op jit(solution)/shard_map/while/body/eval_jaxpr/vmap()/gather | solution.py:29
  415.3 6.5 %fusion.35 = f32[8,8,240,128]{3,2,1,0:T(8,128)} fusion(f32[8,8,240,128]{3,2,1,0:T(8,128)} %get-tuple-element.153, s32[]{:T(128)} %get-tuple-element.152, bf16[8,16,240,128]{3,2,1,0:T(8,128)(2,1)} %bitcast.48, f32[8,16,128]{2,1,0:T(8,128)S(1)} %broadcast_multiply_fusion.4), kind=kOutput, calls=%fused_computation.15.clone.1 | convolution fusion | flops 1017118720 | bytes 8913408 | tf_op jit(solution)/shard_map/while/body/eval_jaxpr/vmap(kgj,kjt->gt)/dot_general | solution.py:30
  421.9 1.3 gather_fusion.1
  423.3 1.0 dynamic-slice_bitcast_fusion.2
  425.3 1.3 gather_fusion.3
  426.7 10.4 %gather_fusion = bf16[128,240,128]{2,1,0:T(8,128)(2,1)} fusion(bf16[160,240,128]{2,1,0:T(8,128)(2,1)} %get-tuple-element.163, s32[1024]{0:T(1024)S(1)} %pad_clamp_fusion.2), kind=kCustom, calls=%fused_computation.clone.clone.1 | custom fusion | bytes 15729152 | tf_op jit(solution)/shard_map/while/body/eval_jaxpr/vmap()/gather | solution.py:29
  437.2 6.5 %fusion.35 = f32[8,8,240,128]{3,2,1,0:T(8,128)} fusion(f32[8,8,240,128]{3,2,1,0:T(8,128)} %get-tuple-element.153, s32[]{:T(128)} %get-tuple-element.152, bf16[8,16,240,128]{3,2,1,0:T(8,128)(2,1)} %bitcast.48, f32[8,16,128]{2,1,0:T(8,128)S(1)} %broadcast_multiply_fusion.4), kind=kOutput, calls=%fused_computation.15.clone.1 | convolution fusion | flops 1017118720 | bytes 8913408 | tf_op jit(solution)/shard_map/while/body/eval_jaxpr/vmap(kgj,kjt->gt)/dot_general | solution.py:30
  443.7 1.3 gather_fusion.1
  445.2 1.0 dynamic-slice_bitcast_fusion.2
  446.1 1.0 gather_fusion.2
  447.1 1.3 gather_fusion.3
  448.6 10.4 %gather_fusion = bf16[128,240,128]{2,1,0:T(8,128)(2,1)} fusion(bf16[160,240,128]{2,1,0:T(8,128)(2,1)} %get-tuple-element.163, s32[1024]{0:T(1024)S(1)} %pad_clamp_fusion.2), kind=kCustom, calls=%fused_computation.clone.clone.1 | custom fusion | bytes 15729152 | tf_op jit(solution)/shard_map/while/body/eval_jaxpr/vmap()/gather | solution.py:29
  459.0 6.5 %fusion.35 = f32[8,8,240,128]{3,2,1,0:T(8,128)} fusion(f32[8,8,240,128]{3,2,1,0:T(8,128)} %get-tuple-element.153, s32[]{:T(128)} %get-tuple-element.152, bf16[8,16,240,128]{3,2,1,0:T(8,128)(2,1)} %bitcast.48, f32[8,16,128]{2,1,0:T(8,128)S(1)} %broadcast_multiply_fusion.4), kind=kOutput, calls=%fused_computation.15.clone.1 | convolution fusion | flops 1017118720 | bytes 8913408 | tf_op jit(solution)/shard_map/while/body/eval_jaxpr/vmap(kgj,kjt->gt)/dot_general | solution.py:30
  465.6 1.3 gather_fusion.1
  467.0 1.0 dynamic-slice_bitcast_fusion.2
  469.0 1.3 gather_fusion.3
  470.4 10.4 %gather_fusion = bf16[128,240,128]{2,1,0:T(8,128)(2,1)} fusion(bf16[160,240,128]{2,1,0:T(8,128)(2,1)} %get-tuple-element.163, s32[1024]{0:T(1024)S(1)} %pad_clamp_fusion.2), kind=kCustom, calls=%fused_computation.clone.clone.1 | custom fusion | bytes 15729152 | tf_op jit(solution)/shard_map/while/body/eval_jaxpr/vmap()/gather | solution.py:29
  480.9 6.5 %fusion.35 = f32[8,8,240,128]{3,2,1,0:T(8,128)} fusion(f32[8,8,240,128]{3,2,1,0:T(8,128)} %get-tuple-element.153, s32[]{:T(128)} %get-tuple-element.152, bf16[8,16,240,128]{3,2,1,0:T(8,128)(2,1)} %bitcast.48, f32[8,16,128]{2,1,0:T(8,128)S(1)} %broadcast_multiply_fusion.4), kind=kOutput, calls=%fused_computation.15.clone.1 | convolution fusion | flops 1017118720 | bytes 8913408 | tf_op jit(solution)/shard_map/while/body/eval_jaxpr/vmap(kgj,kjt->gt)/dot_general | solution.py:30
  487.4 1.3 gather_fusion.1
  488.9 1.0 dynamic-slice_bitcast_fusion.2
  490.8 1.3 gather_fusion.3
  492.3 10.4 %gather_fusion = bf16[128,240,128]{2,1,0:T(8,128)(2,1)} fusion(bf16[160,240,128]{2,1,0:T(8,128)(2,1)} %get-tuple-element.163, s32[1024]{0:T(1024)S(1)} %pad_clamp_fusion.2), kind=kCustom, calls=%fused_computation.clone.clone.1 | custom fusion | bytes 15729152 | tf_op jit(solution)/shard_map/while/body/eval_jaxpr/vmap()/gather | solution.py:29
  502.7 6.4 %fusion.35 = f32[8,8,240,128]{3,2,1,0:T(8,128)} fusion(f32[8,8,240,128]{3,2,1,0:T(8,128)} %get-tuple-element.153, s32[]{:T(128)} %get-tuple-element.152, bf16[8,16,240,128]{3,2,1,0:T(8,128)(2,1)} %bitcast.48, f32[8,16,128]{2,1,0:T(8,128)S(1)} %broadcast_multiply_fusion.4), kind=kOutput, calls=%fused_computation.15.clone.1 | convolution fusion | flops 1017118720 | bytes 8913408 | tf_op jit(solution)/shard_map/while/body/eval_jaxpr/vmap(kgj,kjt->gt)/dot_general | solution.py:30
  509.1 4.3 fusion.22
  513.4 2.9 copy.27
  516.4 5.5 %convert_element_type.26 = bf16[4,60,8192]{2,1,0:T(8,128)(2,1)} reshape(bf16[240,8,8,128]{3,2,1,0:T(8,128)(2,1)} %copy.27) | data formatting | bytes 7864320 | tf_op jit(solution)/shard_map/convert_element_type | solution.py:90
  521.9 3.0 convert_reduce_fusion
  524.9 7.1 %copy.28 = bf16[4,60,8192]{2,0,1:T(4,128)(2,1)} copy(bf16[4,60,8192]{2,1,0:T(8,128)(2,1)} %convert_element_type.26) | data formatting | bytes 7864320
  (98 shorter events, 13.6 us)
Async XLA Ops:
  7.2 68.6 %all-gather.5.cloned.1.call-start = ((), (), s32[]{:S(2)}) async-start(), calls=%async_computation.1 | async-start | bytes 2949120 | tf_op jit(solution)/shard_map/all_gather | solution.py:79
  7.9 286.7 %all-gather.3.cloned.1.call-start = ((), (), s32[]{:S(2)}) async-start(), calls=%async_computation | async-start | bytes 7925760 | tf_op jit(solution)/shard_map/all_gather | solution.py:82
  305.5 9.1 %copy-start = (bf16[240,32,128]{2,1,0:T(8,128)(2,1)S(1)}, bf16[240,32,128]{2,1,0:T(8,128)(2,1)}, u32[]{:S(2)}) copy-start(bf16[240,32,128]{2,1,0:T(8,128)(2,1)} %reshape.81) | copy-start | bytes 5898244
  521.9 10.2 %copy-start.1 = (f32[4,4]{1,0:T(4,128)S(1)}, f32[4,4]{1,0:T(4,128)}, u32[]{:S(2)}) copy-start(f32[4,4]{1,0:T(4,128)} %param.25) | copy-start | bytes 196
  521.9 10.2 %copy-start.2 = (s32[8192]{0:T(1024)S(1)}, s32[8192]{0:T(1024)}, u32[]{:S(2)}) copy-start(s32[8192]{0:T(1024)} %param.17) | copy-start | bytes 98308
Sparse Core Ops, SparseCore 0:
  9.8 65.9 all-gather.4
  77.5 217.0 all-gather.2
where the time goes:
time: 542 us; the launch traced here: 540 us
  waiting for transfers between devices  239 us (44%)
  local copies, waits for them, and re-layouts  180 us (33%)
  matrix products  52.4 us (10%)
  blocking collectives  33 us (6%)
  other arithmetic  20.9 us (4%)
  between operations  15.4 us (3%)
    all_gather x1, waiting for transfers between devices, body(): lax.all_gather(coarse_gens, 'pts', axis=2, tiled=True)  214 us
    gather x8, local copies, waits for them, and re-layouts, one_tile(): coef = table[block_ids]  83.5 us
    dot_general x8, matrix products, one_tile(): jnp.einsum('kgj,kjt->gt', coef, phi, preferred_element_type=jnp.float32)  51.7 us
    all_gather x1, waiting for transfers between devices, body(): lax.all_gather(fine_surplus, 'grp', axis=1, tiled=True)  23.6 us
    unnamed x14, local copies, waits for them, and re-layouts  23.3 us
    unnamed x1, blocking collectives  21.5 us
    gather x32, local copies, waits for them, and re-layouts, one_tile(): scaled = scales[:, None] * states_tile[dims_all[block_ids]]  19.1 us
    all_gather x1, blocking collectives, body(): lax.all_gather(coarse_surplus, 'grp', axis=1, tiled=True)  11.4 us
  transfers between devices with their start and end apart: 2, of which 2 were waited for; matrix products, arithmetic and copies ran while one was open for 3% of the time, Pallas kernels for 0%

commit v1 on v0

--- a/solution.py
+++ b/solution.py
@@ -79,7 +79,9 @@
         lax.all_gather(fine_surplus, "grp", axis=1, tiled=True),
     )
     coarse_all, dims_coarse, levels_coarse = (
-        lax.all_gather(coarse_gens, "pts", axis=2, tiled=True),
+        jnp.concatenate(
+            lax.all_to_all(jnp.stack([coarse_gens] * lax.axis_size("pts")), "pts", 0, 0), axis=2
+        ),
         lax.all_gather(coarse_dim, "pts", axis=0, tiled=True),
         lax.all_gather(coarse_level, "pts", axis=0, tiled=True),
     )

time: 542 us -> 503 us (0.928)
  waiting for transfers between devices: 239 us -> 0.68 us
  blocking collectives: 33 us -> 228 us
  starting transfers between devices: 0.08 us -> 13.2 us
  local copies, waits for them, and re-layouts: 180 us -> 172 us
    all_gather x1 -> x0, waiting for transfers between devices: 214 us -> none  [body(): lax.all_gather(coarse_gens, 'pts', axis=2, tiled=True)]
    unnamed x1, blocking collectives: 21.5 us -> 219 us
    all_gather x1, waiting for transfers between devices: 23.6 us -> 0.01 us  [body(): lax.all_gather(fine_surplus, 'grp', axis=1, tiled=True)]
    all_to_all x0 -> x1, starting transfers between devices: none -> 13.1 us  [body(): lax.all_to_all(jnp.stack([coarse_gens] * lax.axis_size('pts')), 'pts', 0, 0)]
    all_gather x1 -> x0, local copies, waits for them, and re-layouts: 10.9 us -> none  [body(): lax.all_gather(coarse_gens, 'pts', axis=2, tiled=True)]
    reshape x2 -> x1, local copies, waits for them, and re-layouts: 11.1 us -> 1.99 us  [to_table(): return gathered.reshape(shocks * gens, nblocks, BS).transpose(1, 0, 2)]
    all_to_all x0 -> x1, local copies, waits for them, and re-layouts: none -> 8.57 us  [body(): lax.all_to_all(jnp.stack([coarse_gens] * lax.axis_size('pts')), 'pts', 0, 0)]
    unnamed x14 -> x26, local copies, waits for them, and re-layouts: 23.3 us -> 22.6 us
  transfers between devices with their start and end apart: 2 -> 2, of which waited for: 2 -> 0; matrix products, arithmetic and copies ran while one was open for 3% -> 2% of each run, Pallas kernels for 0% -> 0%
where the time goes in v1:
time: 503 us; the launch traced here: 500 us
  blocking collectives  228 us (45%)
  local copies, waits for them, and re-layouts  172 us (34%)
  matrix products  52.6 us (10%)
  other arithmetic  17.6 us (3%)
  between operations  15.5 us (3%)
  starting transfers between devices  13.2 us (3%)
    unnamed x1, blocking collectives  219 us
    gather x8, local copies, waits for them, and re-layouts, one_tile(): coef = table[block_ids]  83 us
    dot_general x8, matrix products, one_tile(): jnp.einsum('kgj,kjt->gt', coef, phi, preferred_element_type=jnp.float32)  51.9 us
    unnamed x26, local copies, waits for them, and re-layouts  22.6 us
    gather x32, local copies, waits for them, and re-layouts, one_tile(): scaled = scales[:, None] * states_tile[dims_all[block_ids]]  19.1 us
    all_to_all x1, starting transfers between devices, body(): lax.all_to_all(jnp.stack([coarse_gens] * lax.axis_size('pts')), 'pts', 0, 0)  13.1 us
    gather x8, local copies, waits for them, and re-layouts, one_tile(): levels_all[block_ids].astype(jnp.float32)  10.1 us
  transfers between devices with their start and end apart: 2, of which 0 were waited for; matrix products, arithmetic and copies ran while one was open for 2% of the time, Pallas kernels for 0%

profile of v1, /device:TPU:1, one launch (start us, length us, event | category | flops | bytes accessed | tf_op | source)
XLA Modules:
  0.0 500.4 jit_solution(787861838879649505)
XLA Ops:
  7.2 9.9 %all_gather.12 = bf16[4,60,128]{2,0,1:T(4,128)(2,1)S(1)} all-gather(bf16[4,30,128]{2,0,1:T(4,128)(2,1)} %param.18), channel_id=1, replica_groups=mesh['pts'=128,'grp'=2] {'grp'}, dimensions={1}, use_global_device_ids=true | all-gather | bytes 92160 | tf_op jit(solution)/shard_map/all_gather | solution.py:78
  17.1 5.2 %stack.8 = bf16[128,4,60,128]{3,1,2,0:T(4,128)(2,1)} broadcast(bf16[4,60,128]{2,0,1:T(4,128)(2,1)S(1)} %all_gather.12), dimensions={1,2,3} | broadcast | bytes 7925760 | tf_op jit(solution)/shard_map/stack | solution.py:83
  22.3 13.1 %all-to-all-start = ((bf16[128,4,60,128]{3,1,2,0:T(4,128)(2,1)}), bf16[128,4,60,128]{3,1,2,0:T(4,128)(2,1)}, u32[]{:S(2)}, u32[]{:S(2)}) async-start(bf16[128,4,60,128]{3,1,2,0:T(4,128)(2,1)} %stack.8), calls=%async_computation | async-start | bytes 15728640 | tf_op jit(solution)/shard_map/all_to_all | solution.py:83
  37.5 2.0 copy.40
  41.8 218.5 %all-reduce.2 = (s32[128]{0:T(128)S(1)}, s32[128]{0:T(128)S(1)}) all-reduce(s32[128]{0:T(128)S(1)} %dynamic-update-slice, s32[128]{0:T(128)S(1)} %dynamic-update-slice.1), channel_id=1, replica_groups=mesh['pts'=128,'grp'=2] {'pts'}, use_global_device_ids=true, to_apply=%add | all-reduce | flops 256 | bytes 2048
  260.4 1.4 bitcast_bitcast_fusion
  261.8 2.6 copy.33
  264.4 2.0 reshape.83
  266.4 8.6 %copy.32 = bf16[128,4,60,128]{3,0,2,1:T(8,128)(2,1)} copy(bf16[128,4,60,128]{3,1,2,0:T(4,128)(2,1)} %all-to-all-done) | data formatting | bytes 15728640 | tf_op jit(solution)/shard_map/all_to_all | solution.py:83
  275.0 8.5 %pad_maximum_fusion = bf16[160,240,128]{2,0,1:T(8,128)(2,1)} fusion(bf16[32,240,128]{2,0,1:T(8,128)(2,1)S(1)} %bitcast.54, bf16[128,240,128]{2,0,1:T(8,128)(2,1)} %bitcast.53), kind=kLoop, calls=%fused_computation.27 | loop fusion | flops 19660800 | bytes 19660800 | tf_op jit(solution)/shard_map/concatenate | solution.py:46
  283.5 11.4 %copy.34 = bf16[160,240,128]{2,1,0:T(8,128)(2,1)} copy(bf16[160,240,128]{2,0,1:T(8,128)(2,1)} %pad_maximum_fusion) | data formatting | bytes 19660800
  294.9 174.4 %while.11 = (s32[]{:T(128)}, f32[8,8,240,128]{3,2,1,0:T(8,128)}, s32[8,8,16]{2,1,0:T(8,128)S(1)}, bf16[160,240,128]{2,1,0:T(8,128)(2,1)}, s32[160]{0:T(256)S(1)}...) while((s32[]{:T(128)}, f32[8,8,240,128]{3,2,1,0:T(8,128)}, ...), condition=%wide.region_1.2_spmd.clone, body=%wide.region_0.1_spmd.clone.sunk | while | flops 1017138048 | bytes 25404508 | solution.py:35
  295.0 1.3 gather_fusion.1
  296.4 1.0 dynamic-slice_bitcast_fusion.2
  297.4 1.0 gather_fusion.2
  298.3 1.3 gather_fusion.3
  299.8 10.4 %gather_fusion = bf16[128,240,128]{2,1,0:T(8,128)(2,1)} fusion(bf16[160,240,128]{2,1,0:T(8,128)(2,1)} %get-tuple-element.172, s32[1024]{0:T(1024)S(1)} %pad_clamp_fusion.2), kind=kCustom, calls=%fused_computation.clone.clone.1 | custom fusion | bytes 15729152 | tf_op jit(solution)/shard_map/while/body/eval_jaxpr/vmap()/gather | solution.py:29
  310.2 6.4 %fusion.35 = f32[8,8,240,128]{3,2,1,0:T(8,128)} fusion(f32[8,8,240,128]{3,2,1,0:T(8,128)} %get-tuple-element.162, s32[]{:T(128)} %get-tuple-element.161, bf16[8,16,240,128]{3,2,1,0:T(8,128)(2,1)} %bitcast.52, f32[8,16,128]{2,1,0:T(8,128)S(1)} %broadcast_multiply_fusion.4), kind=kOutput, calls=%fused_computation.15.clone.1 | convolution fusion | flops 1017118720 | bytes 8913408 | tf_op jit(solution)/shard_map/while/body/eval_jaxpr/vmap(kgj,kjt->gt)/dot_general | solution.py:30
  316.7 1.3 gather_fusion.1
  318.2 1.0 dynamic-slice_bitcast_fusion.2
  319.1 1.0 gather_fusion.2
  320.1 1.3 gather_fusion.3
  321.6 10.4 %gather_fusion = bf16[128,240,128]{2,1,0:T(8,128)(2,1)} fusion(bf16[160,240,128]{2,1,0:T(8,128)(2,1)} %get-tuple-element.172, s32[1024]{0:T(1024)S(1)} %pad_clamp_fusion.2), kind=kCustom, calls=%fused_computation.clone.clone.1 | custom fusion | bytes 15729152 | tf_op jit(solution)/shard_map/while/body/eval_jaxpr/vmap()/gather | solution.py:29
  331.9 6.5 %fusion.35 = f32[8,8,240,128]{3,2,1,0:T(8,128)} fusion(f32[8,8,240,128]{3,2,1,0:T(8,128)} %get-tuple-element.162, s32[]{:T(128)} %get-tuple-element.161, bf16[8,16,240,128]{3,2,1,0:T(8,128)(2,1)} %bitcast.52, f32[8,16,128]{2,1,0:T(8,128)S(1)} %broadcast_multiply_fusion.4), kind=kOutput, calls=%fused_computation.15.clone.1 | convolution fusion | flops 1017118720 | bytes 8913408 | tf_op jit(solution)/shard_map/while/body/eval_jaxpr/vmap(kgj,kjt->gt)/dot_general | solution.py:30
  338.5 1.3 gather_fusion.1
  339.9 1.0 dynamic-slice_bitcast_fusion.2
  340.9 1.0 gather_fusion.2
  341.9 1.3 gather_fusion.3
  343.3 10.4 %gather_fusion = bf16[128,240,128]{2,1,0:T(8,128)(2,1)} fusion(bf16[160,240,128]{2,1,0:T(8,128)(2,1)} %get-tuple-element.172, s32[1024]{0:T(1024)S(1)} %pad_clamp_fusion.2), kind=kCustom, calls=%fused_computation.clone.clone.1 | custom fusion | bytes 15729152 | tf_op jit(solution)/shard_map/while/body/eval_jaxpr/vmap()/gather | solution.py:29
  353.7 6.5 %fusion.35 = f32[8,8,240,128]{3,2,1,0:T(8,128)} fusion(f32[8,8,240,128]{3,2,1,0:T(8,128)} %get-tuple-element.162, s32[]{:T(128)} %get-tuple-element.161, bf16[8,16,240,128]{3,2,1,0:T(8,128)(2,1)} %bitcast.52, f32[8,16,128]{2,1,0:T(8,128)S(1)} %broadcast_multiply_fusion.4), kind=kOutput, calls=%fused_computation.15.clone.1 | convolution fusion | flops 1017118720 | bytes 8913408 | tf_op jit(solution)/shard_map/while/body/eval_jaxpr/vmap(kgj,kjt->gt)/dot_general | solution.py:30
  360.3 1.3 gather_fusion.1
  361.7 1.0 dynamic-slice_bitcast_fusion.2
  362.7 1.0 gather_fusion.2
  363.6 1.3 gather_fusion.3
  365.1 10.4 %gather_fusion = bf16[128,240,128]{2,1,0:T(8,128)(2,1)} fusion(bf16[160,240,128]{2,1,0:T(8,128)(2,1)} %get-tuple-element.172, s32[1024]{0:T(1024)S(1)} %pad_clamp_fusion.2), kind=kCustom, calls=%fused_computation.clone.clone.1 | custom fusion | bytes 15729152 | tf_op jit(solution)/shard_map/while/body/eval_jaxpr/vmap()/gather | solution.py:29
  375.5 6.5 %fusion.35 = f32[8,8,240,128]{3,2,1,0:T(8,128)} fusion(f32[8,8,240,128]{3,2,1,0:T(8,128)} %get-tuple-element.162, s32[]{:T(128)} %get-tuple-element.161, bf16[8,16,240,128]{3,2,1,0:T(8,128)(2,1)} %bitcast.52, f32[8,16,128]{2,1,0:T(8,128)S(1)} %broadcast_multiply_fusion.4), kind=kOutput, calls=%fused_computation.15.clone.1 | convolution fusion | flops 1017118720 | bytes 8913408 | tf_op jit(solution)/shard_map/while/body/eval_jaxpr/vmap(kgj,kjt->gt)/dot_general | solution.py:30
  382.1 1.3 gather_fusion.1
  383.5 1.0 dynamic-slice_bitcast_fusion.2
  384.5 1.0 gather_fusion.2
  385.4 1.3 gather_fusion.3
  386.9 10.4 %gather_fusion = bf16[128,240,128]{2,1,0:T(8,128)(2,1)} fusion(bf16[160,240,128]{2,1,0:T(8,128)(2,1)} %get-tuple-element.172, s32[1024]{0:T(1024)S(1)} %pad_clamp_fusion.2), kind=kCustom, calls=%fused_computation.clone.clone.1 | custom fusion | bytes 15729152 | tf_op jit(solution)/shard_map/while/body/eval_jaxpr/vmap()/gather | solution.py:29
  397.3 6.4 %fusion.35 = f32[8,8,240,128]{3,2,1,0:T(8,128)} fusion(f32[8,8,240,128]{3,2,1,0:T(8,128)} %get-tuple-element.162, s32[]{:T(128)} %get-tuple-element.161, bf16[8,16,240,128]{3,2,1,0:T(8,128)(2,1)} %bitcast.52, f32[8,16,128]{2,1,0:T(8,128)S(1)} %broadcast_multiply_fusion.4), kind=kOutput, calls=%fused_computation.15.clone.1 | convolution fusion | flops 1017118720 | bytes 8913408 | tf_op jit(solution)/shard_map/while/body/eval_jaxpr/vmap(kgj,kjt->gt)/dot_general | solution.py:30
  403.8 1.3 gather_fusion.1
  405.3 1.0 dynamic-slice_bitcast_fusion.2
  406.2 1.0 gather_fusion.2
  407.2 1.3 gather_fusion.3
  408.6 10.4 %gather_fusion = bf16[128,240,128]{2,1,0:T(8,128)(2,1)} fusion(bf16[160,240,128]{2,1,0:T(8,128)(2,1)} %get-tuple-element.172, s32[1024]{0:T(1024)S(1)} %pad_clamp_fusion.2), kind=kCustom, calls=%fused_computation.clone.clone.1 | custom fusion | bytes 15729152 | tf_op jit(solution)/shard_map/while/body/eval_jaxpr/vmap()/gather | solution.py:29
  419.0 6.6 %fusion.35 = f32[8,8,240,128]{3,2,1,0:T(8,128)} fusion(f32[8,8,240,128]{3,2,1,0:T(8,128)} %get-tuple-element.162, s32[]{:T(128)} %get-tuple-element.161, bf16[8,16,240,128]{3,2,1,0:T(8,128)(2,1)} %bitcast.52, f32[8,16,128]{2,1,0:T(8,128)S(1)} %broadcast_multiply_fusion.4), kind=kOutput, calls=%fused_computation.15.clone.1 | convolution fusion | flops 1017118720 | bytes 8913408 | tf_op jit(solution)/shard_map/while/body/eval_jaxpr/vmap(kgj,kjt->gt)/dot_general | solution.py:30
  425.7 1.3 gather_fusion.1
  427.1 1.0 dynamic-slice_bitcast_fusion.2
  429.1 1.3 gather_fusion.3
  430.5 10.4 %gather_fusion = bf16[128,240,128]{2,1,0:T(8,128)(2,1)} fusion(bf16[160,240,128]{2,1,0:T(8,128)(2,1)} %get-tuple-element.172, s32[1024]{0:T(1024)S(1)} %pad_clamp_fusion.2), kind=kCustom, calls=%fused_computation.clone.clone.1 | custom fusion | bytes 15729152 | tf_op jit(solution)/shard_map/while/body/eval_jaxpr/vmap()/gather | solution.py:29
  440.9 6.5 %fusion.35 = f32[8,8,240,128]{3,2,1,0:T(8,128)} fusion(f32[8,8,240,128]{3,2,1,0:T(8,128)} %get-tuple-element.162, s32[]{:T(128)} %get-tuple-element.161, bf16[8,16,240,128]{3,2,1,0:T(8,128)(2,1)} %bitcast.52, f32[8,16,128]{2,1,0:T(8,128)S(1)} %broadcast_multiply_fusion.4), kind=kOutput, calls=%fused_computation.15.clone.1 | convolution fusion | flops 1017118720 | bytes 8913408 | tf_op jit(solution)/shard_map/while/body/eval_jaxpr/vmap(kgj,kjt->gt)/dot_general | solution.py:30
  447.5 1.3 gather_fusion.1
  449.0 1.0 dynamic-slice_bitcast_fusion.2
  450.0 1.0 gather_fusion.2
  450.9 1.3 gather_fusion.3
  452.4 10.4 %gather_fusion = bf16[128,240,128]{2,1,0:T(8,128)(2,1)} fusion(bf16[160,240,128]{2,1,0:T(8,128)(2,1)} %get-tuple-element.172, s32[1024]{0:T(1024)S(1)} %pad_clamp_fusion.2), kind=kCustom, calls=%fused_computation.clone.clone.1 | custom fusion | bytes 15729152 | tf_op jit(solution)/shard_map/while/body/eval_jaxpr/vmap()/gather | solution.py:29
  462.8 6.5 %fusion.35 = f32[8,8,240,128]{3,2,1,0:T(8,128)} fusion(f32[8,8,240,128]{3,2,1,0:T(8,128)} %get-tuple-element.162, s32[]{:T(128)} %get-tuple-element.161, bf16[8,16,240,128]{3,2,1,0:T(8,128)(2,1)} %bitcast.52, f32[8,16,128]{2,1,0:T(8,128)S(1)} %broadcast_multiply_fusion.4), kind=kOutput, calls=%fused_computation.15.clone.1 | convolution fusion | flops 1017118720 | bytes 8913408 | tf_op jit(solution)/shard_map/while/body/eval_jaxpr/vmap(kgj,kjt->gt)/dot_general | solution.py:30
  469.2 4.3 fusion.22
  473.5 2.9 copy.36
  476.5 5.5 %convert_element_type.26 = bf16[4,60,8192]{2,1,0:T(8,128)(2,1)} reshape(bf16[240,8,8,128]{3,2,1,0:T(8,128)(2,1)} %copy.36) | data formatting | bytes 7864320 | tf_op jit(solution)/shard_map/convert_element_type | solution.py:92
  482.0 3.0 convert_reduce_fusion
  485.0 7.1 %copy.37 = bf16[4,60,8192]{2,0,1:T(4,128)(2,1)} copy(bf16[4,60,8192]{2,1,0:T(8,128)(2,1)} %convert_element_type.26) | data formatting | bytes 7864320
  (109 shorter events, 8.9 us)
Async XLA Ops:
  22.3 17.2 %copy-start.1 = (s32[64,8]{0,1:T(8,128)S(1)}, s32[64,8]{0,1:T(8,128)}, u32[]{:S(2)}) copy-start(s32[64,8]{0,1:T(8,128)} %param.16) | copy-start | bytes 6148
  22.3 17.2 %copy-start.2 = (s32[64,8]{0,1:T(8,128)S(1)}, s32[64,8]{0,1:T(8,128)}, u32[]{:S(2)}) copy-start(s32[64,8]{0,1:T(8,128)} %param.15) | copy-start | bytes 6148
  22.3 17.3 %copy-start.8 = (u32[256]{0:T(256)S(1)}, u32[256]{0:T(256)}, u32[]{:S(2)}) copy-start(u32[256]{0:T(256)} %constant.67) | copy-start | bytes 3076
  22.3 19.4 %copy-start.3 = (f32[4,4]{1,0:T(4,128)S(1)}, f32[4,4]{1,0:T(4,128)}, u32[]{:S(2)}) copy-start(f32[4,4]{1,0:T(4,128)} %param.25) | copy-start | bytes 196
  22.3 238.1 %copy-start.4 = (s32[32]{0:T(128)S(1)}, s32[32]{0:T(128)}, u32[]{:S(2)}) copy-start(s32[32]{0:T(128)} %param.23) | copy-start | bytes 388
  22.3 238.1 %copy-start.5 = (s32[32]{0:T(128)S(1)}, s32[32]{0:T(128)}, u32[]{:S(2)}) copy-start(s32[32]{0:T(128)} %param.22) | copy-start | bytes 388
  22.3 238.1 %copy-start.7 = (f32[4]{0:T(128)S(1)}, f32[4]{0:T(128)}, u32[]{:S(2)}) copy-start(f32[4]{0:T(128)} %param.24) | copy-start | bytes 52
  22.3 244.1 %all-to-all-start = ((bf16[128,4,60,128]{3,1,2,0:T(4,128)(2,1)}), bf16[128,4,60,128]{3,1,2,0:T(4,128)(2,1)}, u32[]{:S(2)}, u32[]{:S(2)}) async-start(bf16[128,4,60,128]{3,1,2,0:T(4,128)(2,1)} %stack.8), calls=%async_computation | async-start | bytes 15728640 | tf_op jit(solution)/shard_map/all_to_all | solution.py:83
  35.4 226.4 %all-gather.2.cloned.1.call-start = ((), (), s32[]{:S(2)}) async-start(), calls=%async_computation.1 | async-start | bytes 2949120 | tf_op jit(solution)/shard_map/all_gather | solution.py:79
  266.4 8.6 %copy-start = (bf16[240,32,128]{2,1,0:T(8,128)(2,1)S(1)}, bf16[240,32,128]{2,1,0:T(8,128)(2,1)}, u32[]{:S(2)}) copy-start(bf16[240,32,128]{2,1,0:T(8,128)(2,1)} %reshape.83) | copy-start | bytes 5898244
  482.0 10.2 %copy-start.6 = (s32[8192]{0:T(1024)S(1)}, s32[8192]{0:T(1024)}, u32[]{:S(2)}) copy-start(s32[8192]{0:T(1024)} %param.17) | copy-start | bytes 98308
Sparse Core Ops, SparseCore 0:
  38.1 73.4 all-gather.1
